TPU v7x, 256 devices: a whole 4x4x8 slice. The times are simulated.
256 devices in a mesh: guide: 2 (over z_lo), seq: 32 (over x, y, core), tp: 4 (over z_hi).
Axes of the slice: x: 4, y: 4, z: 8 (z_hi: 4, z_lo: 2; z = z_hi * 2 + z_lo), core: 2. Of those that a mesh axis runs over, the one named last changes fastest.
Arguments:
- hidden: bfloat16 [2048, 3072], P('seq', 'tp'), may hold values from -6 to 6
- seg_ids: int32 [2048], P('seq'), may hold values from 0 to 3, never falling along the last dimension, each value on 1 to 769 neighbouring positions
- modulation: bfloat16 [2, 4, 3, 3072], P('guide'), may hold values from -4 to 4
- qk_gain: float32 [2, 128], replicated, may hold values from 0.5 to 5
- w_qkv: bfloat16 [3072, 3, 1536], P(None, None, 'tp'), may hold values from -0.109375 to 0.109375
- w_mlp_in: bfloat16 [3072, 6144], P('seq', 'tp'), may hold values from -0.109375 to 0.109375
- w_out: bfloat16 [1536, 3072], P('tp'), may hold values from -0.5 to 0.5
- w_mlp_back: bfloat16 [3072, 6144], P('seq', 'tp'), may hold values from -0.078125 to 0.078125
Outputs:
- guided: bfloat16 [2048, 4, 2, 384], P('seq', 'tp', 'guide')
Inputs may be any that keep to these rules, and one draw needn't show every extreme that they name: `seg_ids`: 4 requests lie end to end in order; each holds 1 to 769 rows and one holds exactly 769.
All inputs are finite; a program needn't handle non-finite values.
Results may differ from a plain program's by a relative error of at most 0.014.
The roundings to bfloat16 on the way count: a program that leaves them out, or rounds other values in their place, can miss the bound.
Values may be sent and summed in bfloat16 or wider, within the bound.
A program may use at most 128 MiB of HBM per device.

v0:
```python
import jax
import jax.numpy as jnp
from jax import lax
from jax.sharding import PartitionSpec as P

D = 3072
HEAD = 128
guidance = 3.5


def from_partner(block, axis, apart):
    count = lax.axis_size(axis)
    route = []
    for low in range(count):
        high = low | 1 << apart
        if high != low and high < count:
            route += [(low, high), (high, low)]
    return lax.ppermute(block, axis, route)


def head_norm(values, gain):
    return values * lax.rsqrt(jnp.mean(values * values, axis=-1, keepdims=True) + 1e-06) * gain


def on_device(hidden, seg_ids, modulation, qk_gain, w_qkv, w_mlp_in, w_out, w_mlp_back):
    rows = hidden.shape[0]
    local_width = hidden.shape[1]
    group = w_out.shape[0]
    heads_here = group // HEAD
    requests = modulation.shape[1]
    tp_index = lax.axis_index("tp")
    full = lax.all_gather(hidden, "tp", axis=1, tiled=True)
    xf = full.astype(jnp.float32)
    centred = xf - jnp.mean(xf, axis=-1, keepdims=True)
    normed = centred * lax.rsqrt(jnp.mean(centred * centred, axis=-1, keepdims=True) + 1e-06)
    one_hot = (seg_ids[:, None] == lax.iota(jnp.int32, requests)[None, :]).astype(jnp.bfloat16)
    table = modulation[0, :, 0:2, :].reshape(requests, 2 * D)
    looked = jnp.dot(one_hot, table, preferred_element_type=jnp.float32)
    xmod = (normed * (1.0 + looked[:, D:]) + looked[:, :D]).astype(jnp.bfloat16)
    gate_table = lax.dynamic_slice_in_dim(
        modulation[0, :, 2, :], tp_index * local_width, local_width, 1
    )
    gate = jnp.dot(one_hot, gate_table, preferred_element_type=jnp.float32)
    mlp_pre = jnp.dot(
        xmod,
        lax.all_gather(w_mlp_in, "seq", axis=0, tiled=True),
        preferred_element_type=jnp.float32,
    )
    mlp_act = jax.nn.gelu(mlp_pre, approximate=True).astype(jnp.bfloat16)
    proj = jnp.einsum("td,dck->tck", xmod, w_qkv, preferred_element_type=jnp.float32)
    query = head_norm(proj[:, 0].reshape(rows, heads_here, HEAD), qk_gain[0]).astype(jnp.bfloat16)
    key_rows = head_norm(proj[:, 1].reshape(rows, heads_here, HEAD), qk_gain[1]).astype(
        jnp.bfloat16
    )
    value_rows = proj[:, 2].astype(jnp.bfloat16)
    packed = jnp.concatenate([key_rows.reshape(rows, group), value_rows], axis=1)
    seg_plus = seg_ids + 1
    keys_all = lax.all_gather(packed, "seq", axis=0, tiled=True)
    seg_all = lax.all_gather(seg_plus, "seq", axis=0, tiled=True)
    count = keys_all.shape[0]
    keys = keys_all[:, :group].reshape(count, heads_here, HEAD)
    values = keys_all[:, group:].reshape(count, heads_here, HEAD)
    score = jnp.einsum("qhe,khe->hqk", query, keys, preferred_element_type=jnp.float32) * HEAD ** (
        -0.5
    )
    score = jnp.where((seg_plus[:, None] == seg_all[None, :])[None], score, -1e30)
    peak = jnp.max(score, axis=-1, keepdims=True)
    weight = jnp.exp(score - peak)
    total = jnp.sum(weight, axis=-1)
    summed = jnp.einsum(
        "hqk,khe->hqe", weight.astype(jnp.bfloat16), values, preferred_element_type=jnp.float32
    )
    attended = (summed / total[:, :, None]).astype(jnp.bfloat16)
    attended = jnp.transpose(attended, (1, 0, 2)).reshape(rows, group)
    mlp_term = lax.dot_general(
        mlp_act,
        lax.all_gather(w_mlp_back, "seq", axis=0, tiled=True),
        (((1,), (1,)), ((), ())),
        preferred_element_type=jnp.float32,
    )
    partial_term = jnp.dot(attended, w_out, preferred_element_type=jnp.float32) + mlp_term
    branch = lax.psum_scatter(
        partial_term.astype(jnp.bfloat16), "tp", scatter_dimension=1, tiled=True
    ).astype(jnp.float32)
    own_half = (hidden.astype(jnp.float32) + gate * branch).astype(jnp.bfloat16)
    split_width = local_width // 2
    guide_index = lax.axis_index("guide")
    kept = lax.dynamic_slice_in_dim(own_half, guide_index * split_width, split_width, 1)
    handed = lax.dynamic_slice_in_dim(own_half, (1 - guide_index) * split_width, split_width, 1)
    other_half = from_partner(handed, "guide", 0)
    is_cond = guide_index == 0
    cond = jnp.where(is_cond, kept, other_half).astype(jnp.float32)
    uncond = jnp.where(is_cond, other_half, kept).astype(jnp.float32)
    guided = (uncond + guidance * (cond - uncond)).astype(jnp.bfloat16)
    return guided.reshape(rows, 1, 1, split_width)


def solution(mesh):
    in_specs = (
        P("seq", "tp"),
        P("seq"),
        P("guide", None, None, None),
        P(),
        P(None, None, "tp"),
        P("seq", "tp"),
        P("tp", None),
        P("seq", "tp"),
    )
    out_specs = P("seq", "tp", "guide", None)
    return jax.shard_map(
        on_device, mesh=mesh, in_specs=in_specs, out_specs=out_specs, check_vma=False
    )
```

profile of v0, /device:TPU:6, one launch (start us, length us, event | category | flops | bytes accessed | tf_op | source)
XLA Modules:
  0.0 259.2 jit_solution(889151841724916340)
XLA Ops:
  6.5 19.1 %all_gather.16 = bf16[64,3072]{1,0:T(8,128)(2,1)S(1)} all-gather(bf16[64,768]{1,0:T(8,128)(2,1)} %param.8), channel_id=1, replica_groups=mesh['guide'=2,'seq'=32,'tp'=4] {'tp'}, dimensions={1}, use_global_device_ids=true | all-gather | bytes 491520 | tf_op jit(solution)/shard_map/all_gather | solution.py:32
  25.6 0.2 convert_reduce_fusion
  25.8 0.3 fusion.11
  26.1 0.8 slice.35
  26.9 1.1 fusion.42
  28.0 0.2 fusion.14
  28.2 4.3 %fusion.25 = f32[64,3,384]{2,0,1:T(8,128)S(1)} fusion(bf16[3072,3,384]{2,0,1:T(8,128)(2,1)} %param.12, bf16[64,3072]{1,0:T(8,128)(2,1)S(1)} %fusion.14), kind=kOutput, calls=%fused_computation.33 | convolution fusion | flops 452984832 | bytes 7766016 | tf_op jit(solution)/shard_map/td,dck->tck/dot_general | solution.py:50
  32.7 0.1 reduce_sum.48
  33.0 0.7 pad_maximum_fusion
  33.7 0.7 all-gather.6.cloned.1.call-update
  34.5 0.7 all-gather.8.cloned.1.call-update
  35.3 0.6 dynamic-slice.1
  36.7 14.9 %all-reduce = s32[2048]{0:T(1024)S(1)} all-reduce(s32[2048]{0:T(1024)S(1)} %get-tuple-element.12), channel_id=1, replica_groups=mesh['guide'=2,'seq'=32,'tp'=4] {'seq'}, use_global_device_ids=true, to_apply=%add | all-reduce | flops 2048 | bytes 16384
  51.9 0.1 broadcast_compare_fusion
  52.0 30.8 %all-gather.4.cloned.1.call-done = bf16[2048,768]{1,0:T(8,128)(2,1)} async-done(((bf16[64,768]{1,0:T(8,128)(2,1)}), bf16[2048,768]{1,0:T(8,128)(2,1)}) %all-gather.4.cloned.1.call-update) | async-done | bytes 3145744 | tf_op jit(solution)/shard_map/all_gather | solution.py:58
  82.8 3.9 %fusion.53 = (bf16[2048,384]{1,0:T(8,128)(2,1)}, bf16[2048,384]{1,0:T(8,128)(2,1)}) fusion(bf16[2048,768]{1,0:T(8,128)(2,1)} %all-gather.4.cloned.1.call-done), kind=kLoop, calls=%fused_computation.79 | loop fusion | bytes 6291456 | tf_op jit(solution)/shard_map/slice | solution.py:61
  86.7 2.6 %copy.31 = bf16[2048,384]{0,1:T(8,128)(2,1)} copy(bf16[2048,384]{1,0:T(8,128)(2,1)} %get-tuple-element.5) | data formatting | bytes 3145728 | tf_op jit(solution)/shard_map/slice | solution.py:61
  89.3 2.6 %copy.34 = bf16[2048,384]{0,1:T(8,128)(2,1)} copy(bf16[2048,384]{1,0:T(8,128)(2,1)} %get-tuple-element.6) | data formatting | bytes 3145728 | tf_op jit(solution)/shard_map/slice | solution.py:62
  92.0 2.0 fusion.55
  94.0 0.4 fusion.2
  94.3 1.0 copy-done.1
  95.4 0.7 fusion.8
  96.1 0.5 fusion.38
  96.7 49.0 %all-gather.6.cloned.1.call-done = bf16[3072,1536]{1,0:T(8,128)(2,1)} async-done(((bf16[96,1536]{1,0:T(8,128)(2,1)}), bf16[3072,1536]{1,0:T(8,128)(2,1)}) %all-gather.6.cloned.1.call-update) | async-done | bytes 9437200 | tf_op jit(solution)/shard_map/all_gather | solution.py:46
  145.7 62.7 %all-gather.8.cloned.1.call-done = bf16[3072,1536]{1,0:T(8,128)(2,1)} async-done(((bf16[96,1536]{1,0:T(8,128)(2,1)}), bf16[3072,1536]{1,0:T(8,128)(2,1)}) %all-gather.8.cloned.1.call-update) | async-done | bytes 9437200 | tf_op jit(solution)/shard_map/all_gather | solution.py:77
  208.3 11.7 %fusion = bf16[64,3072]{1,0:T(8,128)(2,1)} fusion(f32[64,3072]{1,0:T(8,128)S(1)} %fusion.38, bf16[3072,1536]{1,0:T(8,128)(2,1)} %all-gather.8.cloned.1.call-done, bf16[64,3072]{1,0:T(8,128)(2,1)S(1)} %fusion.14, bf16[3072,1536]{1,0:T(8,128)(2,1)} %all-gather.6.cloned.1.call-done), kind=kOutput, calls=%fused_computation.1 | convolution fusion | flops 1209237504 | bytes 20447232 | tf_op jit(solution)/shard_map/dot_general | solution.py:75
  220.0 0.8 slice.34
  220.8 25.8 %reduce-scatter.2.cloned.1.call-done = bf16[64,768]{1,0:T(8,128)(2,1)} async-done(((bf16[64,3072]{1,0:T(8,128)(2,1)}), bf16[64,768]{1,0:T(8,128)(2,1)}) %reduce-scatter.2.cloned.1.call-update) | async-done | bytes 98320 | tf_op jit(solution)/shard_map/reduce_scatter | solution.py:82
  246.6 1.2 fusion.5
  247.8 0.6 collective-permute-start
  248.4 3.6 %collective-permute-done = bf16[64,384]{1,0:T(8,128)(2,1)S(1)} collective-permute-done((bf16[64,384]{1,0:T(8,128)(2,1)S(1)}, bf16[64,384]{1,0:T(8,128)(2,1)S(1)}, u32[]{:S(2)}, u32[]{:S(2)}) %collective-permute-start) | collective-permute-done | bytes 49184 | tf_op jit(solution)/shard_map/ppermute | solution.py:18
  252.0 0.6 fusion.37
  (32 shorter events, 0.9 us)
Async XLA Ops:
  6.5 89.6 %copy-start = (bf16[384,3072]{1,0:T(8,128)(2,1)S(1)}, bf16[384,3072]{1,0:T(8,128)(2,1)}, u32[]{:S(2)}) copy-start(bf16[384,3072]{1,0:T(8,128)(2,1)} %param.14) | copy-start | bytes 7077892
  6.5 76.3 %all-gather.4.cloned.1.call-start = ((), (), s32[]{:S(2)}) async-start(), calls=%async_computation.1 | async-start | bytes 3244032 | tf_op jit(solution)/shard_map/all_gather | solution.py:58
  28.2 4.6 %copy-start.3 = (f32[2,128]{1,0:T(2,128)S(1)}, f32[2,128]{1,0:T(2,128)}, u32[]{:S(2)}) copy-start(f32[2,128]{1,0:T(2,128)} %param.11) | copy-start | bytes 3076
  32.5 2.7 %copy-start.4 = (u32[256]{0:T(256)S(1)}, u32[256]{0:T(256)}, u32[]{:S(2)}) copy-start(u32[256]{0:T(256)} %constant.55) | copy-start | bytes 3076
  32.5 4.0 %copy-start.2 = (s32[64]{0:T(128)S(1)}, s32[64]{0:T(128)}, u32[]{:S(2)}) copy-start(s32[64]{0:T(128)} %param.9) | copy-start | bytes 772
  33.7 112.0 %all-gather.6.cloned.1.call-start = ((), (), s32[]{:S(2)}) async-start(), calls=%async_computation.2 | async-start | bytes 9732096 | tf_op jit(solution)/shard_map/all_gather | solution.py:46
  34.4 173.9 %all-gather.8.cloned.1.call-start = ((), (), s32[]{:S(2)}) async-start(), calls=%async_computation.3 | async-start | bytes 9732096 | tf_op jit(solution)/shard_map/all_gather | solution.py:77
  35.2 211.4 %reduce-scatter.2.cloned.1.call-start = ((), (), s32[]{:S(2)}) async-start(), calls=%async_computation.4 | async-start | bytes 491520 | tf_op jit(solution)/shard_map/reduce_scatter | solution.py:82
  94.0 1.4 copy-start.1
  247.8 4.2 %collective-permute-start = (bf16[64,384]{1,0:T(8,128)(2,1)S(1)}, bf16[64,384]{1,0:T(8,128)(2,1)S(1)}, u32[]{:S(2)}, u32[]{:S(2)}) collective-permute-start(bf16[64,384]{1,0:T(8,128)(2,1)S(1)} %constant_dynamic-slice_fusion), channel_id=1, source_target_pairs={{0,128},{128,0},{1,129},{129,1},{2,130},{130,2},{3,131},{131,3},{4... | collective-permute-start | bytes 147464 | tf_op jit(solution)/shard_map/ppermute | solution.py:18
Sparse Core Ops, SparseCore 0:
  33.8 48.9 all-gather.3
  85.3 60.2 all-gather.5
  148.2 60.0 all-gather.7
  220.2 26.4 reduce-scatter.1
where the time goes:
time: 260 us; the launch traced here: 259 us
  waiting for transfers between devices  173 us (67%)
  blocking collectives  34 us (13%)
  matrix products  21.4 us (8%)
  between operations  14 us (5%)
  local copies, waits for them, and re-layouts  12.6 us (5%)
  other arithmetic  3.08 us (1%)
    all_gather x1, waiting for transfers between devices, on_device(): lax.all_gather(w_mlp_back, 'seq', axis=0, tiled=True)  62.7 us
    all_gather x1, waiting for transfers between devices, on_device(): lax.all_gather(w_mlp_in, 'seq', axis=0, tiled=True)  49 us
    all_gather x1, waiting for transfers between devices, on_device(): keys_all = lax.all_gather(packed, 'seq', axis=0, tiled=True)  30.8 us
    reduce_scatter x1, waiting for transfers between devices, on_device(): lax.psum_scatter(partial_term.astype(jnp.bfloat16), 'tp', scatter_dimensi...  25.8 us
    all_gather x1, blocking collectives, on_device(): full = lax.all_gather(hidden, 'tp', axis=1, tiled=True)  19.1 us
    unnamed x1, blocking collectives  14.9 us
    dot_general x1, matrix products, on_device(): lax.dot_general(mlp_act, lax.all_gather(w_mlp_back, 'seq', axis=0, tiled=...  11.7 us
    slice x2, local copies, waits for them, and re-layouts, on_device(): keys = keys_all[:, :group].reshape(count, heads_here, HEAD)  6.53 us
  transfers between devices with their start and end apart: 5, of which 5 were waited for; matrix products, arithmetic and copies ran while one was open for 6% of the time, Pallas kernels for 0%

commit v1 on v0

--- a/solution.py
+++ b/solution.py
@@ -1,11 +1,23 @@
+import functools
 import jax
 import jax.numpy as jnp
 from jax import lax
 from jax.sharding import PartitionSpec as P
+from jax.lax import all_to_all, psum
 
 D = 3072
 HEAD = 128
 guidance = 3.5
+
+
+def set_scenes(local_x, a_name, d0):
+    return jnp.concatenate(
+        all_to_all(jnp.stack([local_x for _ in range(psum(1, a_name))], axis=0), a_name, 0, 0),
+        axis=d0,
+    )
+
+
+produce_the_zones = functools.partial(set_scenes, a_name="seq", d0=0)
 
 
 def from_partner(block, axis, apart):
@@ -74,7 +86,7 @@
     attended = jnp.transpose(attended, (1, 0, 2)).reshape(rows, group)
     mlp_term = lax.dot_general(
         mlp_act,
-        lax.all_gather(w_mlp_back, "seq", axis=0, tiled=True),
+        produce_the_zones(w_mlp_back),
         (((1,), (1,)), ((), ())),
         preferred_element_type=jnp.float32,
     )

time: 260 us -> 286 us (1.10)
  blocking collectives: 34 us -> 147 us
  waiting for transfers between devices: 173 us -> 73 us
  starting transfers between devices: 0.68 us -> 8.44 us
  local copies, waits for them, and re-layouts: 12.6 us -> 18.3 us
    unnamed x1, blocking collectives: 14.9 us -> 128 us
    all_gather x1 -> x0, waiting for transfers between devices: 62.7 us -> none  [on_device(): lax.all_gather(w_mlp_back, 'seq', axis=0, tiled=True)]
    all_gather x1, waiting for transfers between devices: 30.8 us -> 0.02 us  [on_device(): keys_all = lax.all_gather(packed, 'seq', axis=0, tiled=True)]
    all_to_all x0 -> x1, starting transfers between devices: none -> 7.78 us  [set_scenes(): all_to_all(jnp.stack([local_x for _ in range(psum(1, a_name))], axis=0),...]
    all_gather x1, waiting for transfers between devices: 49 us -> 42.8 us  [on_device(): lax.all_gather(w_mlp_in, 'seq', axis=0, tiled=True)]
    another operation x0 -> x1, local copies, waits for them, and re-layouts: none -> 5.75 us  [set_scenes(): jnp.stack([local_x for _ in range(psum(1, a_name))], axis=0)]
  transfers between devices with their start and end apart: 5 -> 5, of which waited for: 5 -> 3; matrix products, arithmetic and copies ran while one was open for 6% -> 7% of each run, Pallas kernels for 0% -> 0%
where the time goes in v1:
time: 286 us; the launch traced here: 285 us
  blocking collectives  147 us (51%)
  waiting for transfers between devices  73 us (26%)
  matrix products  21.5 us (8%)
  local copies, waits for them, and re-layouts  18.3 us (6%)
  between operations  14 us (5%)
  starting transfers between devices  8.44 us (3%)
  other arithmetic  3.06 us (1%)
    unnamed x1, blocking collectives  128 us
    all_gather x1, waiting for transfers between devices, on_device(): lax.all_gather(w_mlp_in, 'seq', axis=0, tiled=True)  42.8 us
    reduce_scatter x1, waiting for transfers between devices, on_device(): lax.psum_scatter(partial_term.astype(jnp.bfloat16), 'tp', scatter_dimensi...  25.8 us
    all_gather x1, blocking collectives, on_device(): full = lax.all_gather(hidden, 'tp', axis=1, tiled=True)  19.1 us
    dot_general x1, matrix products, on_device(): lax.dot_general(mlp_act, produce_the_zones(w_mlp_back), (((1,), (1,)), ((...  11.7 us
    all_to_all x1, starting transfers between devices, set_scenes(): all_to_all(jnp.stack([local_x for _ in range(psum(1, a_name))], axis=0),...  7.78 us
    slice x2, local copies, waits for them, and re-layouts, on_device(): keys = keys_all[:, :group].reshape(count, heads_here, HEAD)  6.49 us
    another operation x1, local copies, waits for them, and re-layouts, set_scenes(): jnp.stack([local_x for _ in range(psum(1, a_name))], axis=0)  5.75 us
  transfers between devices with their start and end apart: 5, of which 3 were waited for; matrix products, arithmetic and copies ran while one was open for 7% of the time, Pallas kernels for 0%

profile of v1, /device:TPU:6, one launch (start us, length us, event | category | flops | bytes accessed | tf_op | source)
XLA Modules:
  0.0 285.0 jit_solution(3949629765620992939)
XLA Ops:
  6.5 19.1 %all_gather.13 = bf16[64,3072]{1,0:T(8,128)(2,1)S(1)} all-gather(bf16[64,768]{1,0:T(8,128)(2,1)} %param.8), channel_id=1, replica_groups=mesh['guide'=2,'seq'=32,'tp'=4] {'tp'}, dimensions={1}, use_global_device_ids=true | all-gather | bytes 491520 | tf_op jit(solution)/shard_map/all_gather | solution.py:44
  25.6 0.2 convert_reduce_fusion
  25.8 0.3 fusion.11
  26.1 0.8 slice.35
  26.9 1.1 fusion.42
  28.0 0.2 fusion.14
  28.2 4.3 %fusion.25 = f32[64,3,384]{2,0,1:T(8,128)S(1)} fusion(bf16[3072,3,384]{2,0,1:T(8,128)(2,1)} %param.12, bf16[64,3072]{1,0:T(8,128)(2,1)S(1)} %fusion.14), kind=kOutput, calls=%fused_computation.33 | convolution fusion | flops 452984832 | bytes 7766016 | tf_op jit(solution)/shard_map/td,dck->tck/dot_general | solution.py:62
  32.6 0.1 reduce_sum.48
  33.0 0.6 pad_maximum_fusion
  33.7 0.7 all-gather.5.cloned.1.call-update
  34.4 5.8 %stack.2 = bf16[32,96,1536]{2,1,0:T(8,128)(2,1)} broadcast(bf16[96,1536]{1,0:T(8,128)(2,1)} %param.15), dimensions={1,2} | broadcast | bytes 9732096 | tf_op jit(solution)/shard_map/stack | solution.py:15
  40.1 7.8 %all-to-all-start = ((bf16[32,96,1536]{2,1,0:T(8,128)(2,1)}), bf16[32,96,1536]{2,1,0:T(8,128)(2,1)}, u32[]{:S(2)}, u32[]{:S(2)}) async-start(bf16[32,96,1536]{2,1,0:T(8,128)(2,1)} %stack.2), calls=%async_computation | async-start | bytes 18874368 | tf_op jit(solution)/shard_map/all_to_all | solution.py:15
  48.1 0.6 dynamic-slice.1
  49.4 127.7 %all-reduce = s32[2048]{0:T(1024)S(1)} all-reduce(s32[2048]{0:T(1024)S(1)} %get-tuple-element.12), channel_id=1, replica_groups=mesh['guide'=2,'seq'=32,'tp'=4] {'seq'}, use_global_device_ids=true, to_apply=%add | all-reduce | flops 2048 | bytes 16384
  177.1 0.1 multiply_reduce_fusion
  177.4 0.1 broadcast_compare_fusion
  177.6 3.9 %fusion.53 = (bf16[2048,384]{1,0:T(8,128)(2,1)}, bf16[2048,384]{1,0:T(8,128)(2,1)}) fusion(bf16[2048,768]{1,0:T(8,128)(2,1)} %all-gather.3.cloned.1.call-done), kind=kLoop, calls=%fused_computation.79 | loop fusion | bytes 6291456 | tf_op jit(solution)/shard_map/slice | solution.py:73
  181.5 2.6 copy.31
  184.1 2.6 copy.34
  186.7 2.0 fusion.55
  188.7 0.4 fusion.2
  189.1 1.0 copy-done.1
  190.1 0.7 fusion.8
  190.9 0.5 fusion.38
  191.4 42.8 %all-gather.5.cloned.1.call-done = bf16[3072,1536]{1,0:T(8,128)(2,1)} async-done(((bf16[96,1536]{1,0:T(8,128)(2,1)}), bf16[3072,1536]{1,0:T(8,128)(2,1)}) %all-gather.5.cloned.1.call-update) | async-done | bytes 9437200 | tf_op jit(solution)/shard_map/all_gather | solution.py:58
  234.2 11.7 %fusion = bf16[64,3072]{1,0:T(8,128)(2,1)} fusion(f32[64,3072]{1,0:T(8,128)S(1)} %fusion.38, bf16[3072,1536]{1,0:T(8,128)(2,1)} %bitcast.13, bf16[64,3072]{1,0:T(8,128)(2,1)S(1)} %fusion.14, bf16[3072,1536]{1,0:T(8,128)(2,1)} %all-gather.5.cloned.1.call-done), kind=kOutput, calls=%fused_computation.1 | convolution fusion | flops 1209237504 | bytes 20447232 | tf_op jit(solution)/shard_map/dot_general | solution.py:87
  245.9 0.8 slice.34
  246.7 25.8 %reduce-scatter.2.cloned.1.call-done = bf16[64,768]{1,0:T(8,128)(2,1)} async-done(((bf16[64,3072]{1,0:T(8,128)(2,1)}), bf16[64,768]{1,0:T(8,128)(2,1)}) %reduce-scatter.2.cloned.1.call-update) | async-done | bytes 98320 | tf_op jit(solution)/shard_map/reduce_scatter | solution.py:94
  272.5 1.2 fusion.5
  273.7 0.6 collective-permute-start
  274.2 3.6 %collective-permute-done = bf16[64,384]{1,0:T(8,128)(2,1)S(1)} collective-permute-done((bf16[64,384]{1,0:T(8,128)(2,1)S(1)}, bf16[64,384]{1,0:T(8,128)(2,1)S(1)}, u32[]{:S(2)}, u32[]{:S(2)}) %collective-permute-start) | collective-permute-done | bytes 49184 | tf_op jit(solution)/shard_map/ppermute | solution.py:30
  277.9 0.6 fusion.37
  (32 shorter events, 0.7 us)
Async XLA Ops:
  6.5 184.3 %copy-start = (bf16[384,3072]{1,0:T(8,128)(2,1)S(1)}, bf16[384,3072]{1,0:T(8,128)(2,1)}, u32[]{:S(2)}) copy-start(bf16[384,3072]{1,0:T(8,128)(2,1)} %param.14) | copy-start | bytes 7077892
  6.5 171.1 %all-gather.3.cloned.1.call-start = ((), (), s32[]{:S(2)}) async-start(), calls=%async_computation.2 | async-start | bytes 3244032 | tf_op jit(solution)/shard_map/all_gather | solution.py:70
  28.2 4.6 %copy-start.3 = (f32[2,128]{1,0:T(2,128)S(1)}, f32[2,128]{1,0:T(2,128)}, u32[]{:S(2)}) copy-start(f32[2,128]{1,0:T(2,128)} %param.11) | copy-start | bytes 3076
  33.6 200.6 %all-gather.5.cloned.1.call-start = ((), (), s32[]{:S(2)}) async-start(), calls=%async_computation.3 | async-start | bytes 9732096 | tf_op jit(solution)/shard_map/all_gather | solution.py:58
  40.1 7.9 %copy-start.4 = (u32[256]{0:T(256)S(1)}, u32[256]{0:T(256)}, u32[]{:S(2)}) copy-start(u32[256]{0:T(256)} %constant.55) | copy-start | bytes 3076
  40.1 9.2 %copy-start.2 = (s32[64]{0:T(128)S(1)}, s32[64]{0:T(128)}, u32[]{:S(2)}) copy-start(s32[64]{0:T(128)} %param.9) | copy-start | bytes 772
  40.1 151.3 %all-to-all-start = ((bf16[32,96,1536]{2,1,0:T(8,128)(2,1)}), bf16[32,96,1536]{2,1,0:T(8,128)(2,1)}, u32[]{:S(2)}, u32[]{:S(2)}) async-start(bf16[32,96,1536]{2,1,0:T(8,128)(2,1)} %stack.2), calls=%async_computation | async-start | bytes 18874368 | tf_op jit(solution)/shard_map/all_to_all | solution.py:15
  47.9 224.5 %reduce-scatter.2.cloned.1.call-start = ((), (), s32[]{:S(2)}) async-start(), calls=%async_computation.4 | async-start | bytes 491520 | tf_op jit(solution)/shard_map/reduce_scatter | solution.py:94
  188.7 1.4 copy-start.1
  273.7 4.2 %collective-permute-start = (bf16[64,384]{1,0:T(8,128)(2,1)S(1)}, bf16[64,384]{1,0:T(8,128)(2,1)S(1)}, u32[]{:S(2)}, u32[]{:S(2)}) collective-permute-start(bf16[64,384]{1,0:T(8,128)(2,1)S(1)} %constant_dynamic-slice_fusion), channel_id=1, source_target_pairs={{0,128},{128,0},{1,129},{129,1},{2,130},{130,2},{3,131},{131,3},{4... | collective-permute-start | bytes 147464 | tf_op jit(solution)/shard_map/ppermute | solution.py:30
Sparse Core Ops, SparseCore 0:
  33.8 140.3 all-gather.2
  176.8 57.4 all-gather.4
  246.1 26.3 reduce-scatter.1
